TPU v7x, 32 devices: a whole 2x2x4 slice. The times are simulated.
32 devices in a mesh: ctx: 8 (over y, x, core), mp: 4 (over z).
Axes of the slice: x: 2, y: 2, z: 4, core: 2. Of those that a mesh axis runs over, the one named last changes fastest.
Arguments:
- resid_in: bfloat16 [4096, 8192], P('ctx', 'mp'), may hold values from -6 to 6
- q_mr: bfloat16 [4096, 8192], P('ctx', 'mp'), may hold values from -6 to 6
- k_mr: bfloat16 [4096, 8192], P('ctx', 'mp'), may hold values from -6 to 6
- v_mr: bfloat16 [4096, 8192], P('ctx', 'mp'), may hold values from -6 to 6
- mr_filter: float32 [128, 8192], P(None, 'mp'), may hold values from -0.5 to 0.5
- mr_out: bfloat16 [8192, 8192], P('ctx', 'mp'), may hold values from -0.0625 to 0.0625
- q_li: bfloat16 [4096, 8192], P('ctx', 'mp'), may hold values from -6 to 6
- k_li: bfloat16 [4096, 8192], P('ctx', 'mp'), may hold values from -6 to 6
- li_rate: float32 [8192], P('mp'), may hold values from 2.4414063e-05 to 0.0333333333
- li_residue: float32 [8192], P('mp'), may hold values from 0.5 to 2
Outputs:
- mixed: bfloat16 [4096, 8192], P('ctx', 'mp')
- long_out: bfloat16 [4096, 8192], P('ctx', 'mp')
All inputs are finite; a program needn't handle non-finite values.
Results may differ from a plain program's by a relative error of at most 0.008.
Values may be sent and summed in bfloat16 or wider, within the bound.
A program may use at most 192 MiB of HBM per device.

v0:
```python
import jax
import jax.numpy as jnp
from jax import lax
from jax.sharding import PartitionSpec as P


def passed_along(value, axis, by):
    peers = lax.axis_size(axis)
    pairs = [(i, i + by) for i in range(peers) if 0 <= i + by < peers]
    return lax.ppermute(value, axis, pairs)


def carried_in(value, axis, join, neutral):
    count, mine = (lax.axis_size(axis), lax.axis_index(axis))
    pieces = jax.tree.map(lambda part: lax.all_gather(part, axis), value)
    subtotal = jax.tree.map(
        lambda part, zero: jnp.full_like(part, 0) + jnp.asarray(zero, part.dtype), value, neutral
    )

    def step(position, subtotal):
        longer = join(subtotal, jax.tree.map(lambda part: part[position], pieces))
        return jax.tree.map(lambda new, old: jnp.where(position < mine, new, old), longer, subtotal)

    return lax.fori_loop(0, count - 1, step, subtotal)


def link_pair(earlier, later):
    return (earlier[0] * later[0], later[0] * earlier[1] + later[1])


def body(resid_in, q_mr, k_mr, v_mr, mr_filter, mr_out, q_li, k_li, li_rate, li_residue):
    row_count = q_mr.shape[0]
    chan_count = q_mr.shape[1]
    tap_count = mr_filter.shape[0]
    drive_mr = (k_mr.astype(jnp.float32) * v_mr.astype(jnp.float32)).astype(jnp.bfloat16)
    prev_rows = passed_along(drive_mr[row_count - (tap_count - 1) :], "ctx", 1)
    padded = jnp.concatenate([prev_rows, drive_mr], 0).astype(jnp.float32)[None]
    kernel = mr_filter[::-1][:, None, :]
    filtered = lax.conv_general_dilated(
        padded,
        kernel,
        (1,),
        "VALID",
        dimension_numbers=("NWC", "WIO", "NWC"),
        feature_group_count=chan_count,
        precision=lax.Precision.HIGHEST,
    )[0]
    gated = (q_mr.astype(jnp.float32) * filtered).astype(jnp.bfloat16)
    gathered = lax.all_gather(gated, "mp", axis=1, tiled=True)
    all_rows = lax.all_gather(mr_out, "ctx", axis=0, tiled=True)
    summed = jnp.dot(gathered, all_rows, preferred_element_type=jnp.float32)
    mixed = (resid_in.astype(jnp.float32) + summed).astype(jnp.bfloat16)
    decay = jnp.exp(-li_rate)
    drive_li = k_li.astype(jnp.float32) * mixed.astype(jnp.float32)
    decay_rows = jnp.broadcast_to(decay[None, :], drive_li.shape)
    _, local_state = lax.associative_scan(link_pair, (decay_rows, drive_li), axis=0)
    offsets = jnp.arange(1, row_count + 1, dtype=jnp.float32)[:, None]
    powers = jnp.exp(-li_rate[None, :] * offsets)
    block_end = local_state[row_count - 1]
    block_decay = jnp.exp(-li_rate * row_count)
    identity = (jnp.ones_like(block_decay), jnp.zeros_like(block_end))
    prefix = carried_in((block_decay, block_end), "ctx", link_pair, identity)
    carried = prefix[1]
    state = local_state + powers * carried[None, :]
    scale = li_residue * jnp.sqrt(-jnp.expm1(-2.0 * li_rate))
    long_out = (q_li.astype(jnp.float32) * scale * state).astype(jnp.bfloat16)
    return (mixed, long_out)


def solution(mesh):
    in_specs = (
        P("ctx", "mp"),
        P("ctx", "mp"),
        P("ctx", "mp"),
        P("ctx", "mp"),
        P(None, "mp"),
        P("ctx", "mp"),
        P("ctx", "mp"),
        P("ctx", "mp"),
        P("mp"),
        P("mp"),
    )
    out_specs = (P("ctx", "mp"), P("ctx", "mp"))
    return jax.shard_map(body, mesh=mesh, in_specs=in_specs, out_specs=out_specs, check_vma=False)
```

profile of v0, /device:TPU:0, one launch (start us, length us, event | category | flops | bytes accessed | tf_op | source)
XLA Modules:
  0.0 563.9 jit_solution(2799196935869276048)
XLA Ops:
  7.2 3.1 multiply_convert_fusion.1
  10.3 0.9 slice.256
  11.2 3.2 collective-permute-start
  14.4 5.2 rev.3
  19.6 1.8 maximum_bitcast_fusion
  21.4 45.6 %fusion = f32[1,512,2048]{2,0,1:T(1,128)S(1)} fusion(bf16[1,639,2048]{2,1,0:T(8,128)(2,1)S(1)} %maximum_bitcast_fusion, f32[128,1,2048]{2,0,1:T(8,128)S(1)} %bitcast.22), kind=kOutput, calls=%fused_computation.3 | convolution fusion | flops 1610612736 | bytes 7860224 | tf_op jit(solution)/shard_map/conv_general_dilated | solution.py:39
  67.0 2.9 fusion.2
  71.4 14.1 %all-gather = f32[16384]{0:T(1024)S(1)} all-gather(f32[2048]{0:T(1024)S(1)} %get-tuple-element.139), channel_id=2, replica_groups=mesh['ctx'=8,'mp'=4] {'ctx'}, dimensions={0}, use_global_device_ids=true | all-gather | bytes 73728 | tf_op jit(solution)/shard_map/all_gather | solution.py:15
  86.8 138.0 %all-gather.5.cloned.1.call-done = bf16[512,8192]{1,0:T(8,128)(2,1)} async-done(((bf16[512,2048]{1,0:T(8,128)(2,1)}), bf16[512,8192]{1,0:T(8,128)(2,1)}) %all-gather.5.cloned.1.call-update) | async-done | bytes 8388624 | tf_op jit(solution)/shard_map/all_gather | solution.py:49
  224.8 160.9 %all-gather.7.cloned.1.call-done = bf16[8192,2048]{1,0:T(8,128)(2,1)} async-done(((bf16[1024,2048]{1,0:T(8,128)(2,1)}), bf16[8192,2048]{1,0:T(8,128)(2,1)}) %all-gather.7.cloned.1.call-update) | async-done | bytes 33554448 | tf_op jit(solution)/shard_map/all_gather | solution.py:50
  385.6 25.6 %convert_multiply_fusion = (f32[512,2048]{1,0:T(8,128)}, bf16[512,2048]{1,0:T(8,128)(2,1)}) fusion(bf16[512,2048]{1,0:T(8,128)(2,1)} %param.19, bf16[512,8192]{1,0:T(8,128)(2,1)} %all-gather.5.cloned.1.call-done, bf16[8192,2048]{1,0:T(8,128)(2,1)} %all-gather.7.cloned.1.call-done, bf16[512,2048]{1,0:T(8,128)(2,1)} %param.12), kind=kOutput, calls=%fused_computation.8 | convolution fusion | flops 17186160640 | bytes 52428800 | tf_op jit(solution)/shard_map/dot_general | solution.py:51
  411.3 10.0 %slice.254 = f32[255,2048]{1,0:T(8,128)} slice(f32[512,2048]{1,0:T(8,128)} %get-tuple-element.143), slice={[2:512:2], [0:2048:1]} | slice | bytes 4177920 | tf_op jit(solution)/shard_map/slice | solution.py:56
  421.3 9.8 %slice.200 = f32[256,2048]{1,0:T(8,128)} slice(f32[512,2048]{1,0:T(8,128)} %get-tuple-element.143), slice={[1:512:2], [0:2048:1]} | slice | bytes 4194304 | tf_op jit(solution)/shard_map/slice | solution.py:56
  431.1 9.8 %slice.199 = f32[256,2048]{1,0:T(8,128)} slice(f32[512,2048]{1,0:T(8,128)} %get-tuple-element.143), slice={[0:511:2], [0:2048:1]} | slice | bytes 4194304 | tf_op jit(solution)/shard_map/slice | solution.py:56
  440.9 2.6 multiply_add_fusion
  443.5 2.9 slice.205
  446.4 2.8 slice.204
  449.3 1.7 multiply_add_fusion.1
  450.9 1.7 slice.250
  452.7 1.5 slice.210
  454.1 1.5 slice.209
  455.6 2.1 multiply_add_fusion.2
  457.7 1.7 slice.215
  459.4 1.7 slice.214
  461.1 1.1 multiply_add_fusion.3
  464.2 1.0 multiply_add_fusion.4
  466.5 1.5 multiply_add_fusion.5
  468.0 1.5 slice.242
  469.5 1.5 slice.230
  471.0 1.4 slice.229
  472.4 1.4 multiply_add_fusion.6
  473.8 1.4 slice.235
  475.2 1.4 slice.234
  478.4 1.1 slice.248
  479.6 3.0 slice.252
  482.6 1.4 slice.257
  489.3 0.9 copy-done.2
  490.2 1.1 add.181
  491.3 4.2 pad.70
  495.6 1.8 fusion.4
  497.4 4.9 pad.69
  502.3 3.4 add.183
  506.4 1.5 pad_maximum_fusion
  507.9 16.7 %pad.71 = f32[512,2048]{1,0:T(8,128)} pad(f32[256,2048]{1,0:T(8,128)} %pad_maximum_fusion, f32[]{:T(128)} %constant.35.clone.1), padding=0_1_1x0_0_0 | pad | bytes 6291460 | tf_op jit(solution)/shard_map/pad | solution.py:56
  524.7 9.1 %pad.72 = f32[512,2048]{1,0:T(8,128)} pad(f32[256,2048]{1,0:T(8,128)S(1)} %copy-done.3, f32[]{:T(128)} %constant.35.clone.1), padding=1_0_1x0_0_0 | pad | bytes 6291460 | tf_op jit(solution)/shard_map/pad | solution.py:56
  534.6 9.2 %all-gather.1 = f32[8,1,2048]{2,1,0:T(1,128)S(1)} all-gather(f32[1,1,2048]{2,1,0:T(1,128)S(1)} %add_bitcast_fusion), channel_id=1, replica_groups=mesh['ctx'=8,'mp'=4] {'ctx'}, dimensions={0}, use_global_device_ids=true | all-gather | bytes 73728 | tf_op jit(solution)/shard_map/all_gather | solution.py:15
  543.8 6.3 %while.14 = (s32[]{:T(128)}, f32[2048]{0:T(1024)S(1)}, s32[]{:T(128)}, f32[8,2048]{1,0:T(8,128)}, f32[8,2048]{1,0:T(8,128)S(1)}, /*index=5*/s32[]{:T(128)}, s32[]{:T(128)}) while((s32[]{:T(128)}, f32[2048]{0:T(1024)S(1)}, s32[]{:T(128)}, f32[8,2048]{1,0:T(8,128)}, f32[8,2048]{1,0:T(8,128)S(1)}, /*index=5*/s32[]{:T(128)}, ...), condition=%wide.region_1.2_spmd.clone, body=%wide.region_0.1_spmd.clone.sunk | while | flops 8196 | bytes 65645 | solution.py:24
  550.2 6.9 %multiply_convert_fusion = bf16[512,2048]{1,0:T(8,128)(2,1)} fusion(f32[512,2048]{1,0:T(8,128)} %pad.71, f32[512,2048]{1,0:T(8,128)} %pad.72, bf16[512,2048]{1,0:T(8,128)(2,1)} %param.18, f32[2048]{0:T(1024)S(1)} %get-tuple-element.96, f32[512]{0:T(512)S(1)} %copy-done.28, f32[2048]{0:T(1024)S(1)} %copy-done.24, f32[2048]{0:T(1024)S(1)} %copy-done.23), kind=kLoop, calls=%fused_computation.7 | loop fusion | flops 8388608 | bytes 12609536 | tf_op jit(solution)/shard_map/convert_element_type | solution.py:66
  (136 shorter events, 20.7 us)
Async XLA Ops:
  7.2 7.2 %copy-start.8 = (f32[128,2048]{1,0:T(8,128)S(1)}, f32[128,2048]{1,0:T(8,128)}, u32[]{:S(2)}) copy-start(f32[128,2048]{1,0:T(8,128)} %param.16) | copy-start | bytes 3145732
  7.2 217.6 %all-gather.5.cloned.1.call-start = ((), (), s32[]{:S(2)}) async-start(), calls=%async_computation | async-start | bytes 10485760 | tf_op jit(solution)/shard_map/all_gather | solution.py:49
  11.2 8.3 %collective-permute-start = (bf16[127,2048]{1,0:T(8,128)(2,1)}, bf16[127,2048]{1,0:T(8,128)(2,1)}, u32[]{:S(2)}, u32[]{:S(2)}) collective-permute-start(bf16[127,2048]{1,0:T(8,128)(2,1)} %slice.256), channel_id=1, source_target_pairs={{0,4},{4,8},{8,12},{12,16},{16,20},{20,24},{24,28},{1,5},{5,9},{9,... | collective-permute-start | bytes 1560584 | tf_op jit(solution)/shard_map/ppermute | solution.py:10
  19.6 1.8 copy-start.9
  21.4 45.6 %copy-start.7 = (bf16[512,2048]{1,0:T(8,128)(2,1)S(1)}, bf16[512,2048]{1,0:T(8,128)(2,1)}, u32[]{:S(2)}) copy-start(bf16[512,2048]{1,0:T(8,128)(2,1)} %param.13) | copy-start | bytes 6291460
  69.9 0.8 copy-start.29
  69.9 0.8 copy-start.30
  69.9 315.7 %all-gather.7.cloned.1.call-start = ((), (), s32[]{:S(2)}) async-start(), calls=%async_computation.1 | async-start | bytes 37748736 | tf_op jit(solution)/shard_map/all_gather | solution.py:50
  71.3 369.6 %copy-start.12 = (f32[2048]{0:T(1024)}, f32[2048]{0:T(1024)S(1)}, u32[]{:S(2)}) copy-start(f32[2048]{0:T(1024)S(1)} %get-tuple-element.138) | copy-start | bytes 24580
  71.3 377.9 %copy-start.14 = (f32[2048]{0:T(1024)}, f32[2048]{0:T(1024)S(1)}, u32[]{:S(2)}) copy-start(f32[2048]{0:T(1024)S(1)} %get-tuple-element.141) | copy-start | bytes 24580
  71.3 384.2 %copy-start.16 = (f32[2048]{0:T(1024)}, f32[2048]{0:T(1024)S(1)}, u32[]{:S(2)}) copy-start(f32[2048]{0:T(1024)S(1)} %get-tuple-element.140) | copy-start | bytes 24580
  71.3 389.7 %copy-start.18 = (f32[2048]{0:T(1024)}, f32[2048]{0:T(1024)S(1)}, u32[]{:S(2)}) copy-start(f32[2048]{0:T(1024)S(1)} %get-tuple-element.132) | copy-start | bytes 24580
  71.4 392.9 %copy-start.20 = (f32[2048]{0:T(1024)}, f32[2048]{0:T(1024)S(1)}, u32[]{:S(2)}) copy-start(f32[2048]{0:T(1024)S(1)} %get-tuple-element.133) | copy-start | bytes 24580
  443.5 39.1 %copy-start.1 = (f32[256,2048]{1,0:T(8,128)}, f32[256,2048]{1,0:T(8,128)S(1)}, u32[]{:S(2)}) copy-start(f32[256,2048]{1,0:T(8,128)S(1)} %multiply_add_fusion) | copy-start | bytes 6291460
  450.9 28.6 %copy-start.5 = (f32[128,2048]{1,0:T(8,128)}, f32[128,2048]{1,0:T(8,128)S(1)}, u32[]{:S(2)}) copy-start(f32[128,2048]{1,0:T(8,128)S(1)} %multiply_add_fusion.1) | copy-start | bytes 3145732
  468.0 19.3 %slice-start.3 = ((f32[8,2048]{1,0:T(8,128)}), f32[1,2048]{1,0:T(1,128)S(1)}, s32[]{:S(2)}) async-start(f32[8,2048]{1,0:T(8,128)} %multiply_add_fusion.5), calls=%async_computation.5 | async-start | bytes 16384 | tf_op jit(solution)/shard_map/slice | solution.py:56
  477.8 9.8 %copy-start.10 = (f32[15,2048]{1,0:T(8,128)S(1)}, f32[15,2048]{1,0:T(8,128)}, u32[]{:S(2)}) copy-start(f32[15,2048]{1,0:T(8,128)} %slice.246) | copy-start | bytes 368644
  479.5 7.9 %copy-start.11 = (f32[7,2048]{1,0:T(8,128)S(1)}, f32[7,2048]{1,0:T(8,128)}, u32[]{:S(2)}) copy-start(f32[7,2048]{1,0:T(8,128)} %slice.244) | copy-start | bytes 172036
  479.6 7.9 %copy-start.22 = (f32[2048]{0:T(1024)S(1)}, f32[2048]{0:T(1024)}, u32[]{:S(2)}) copy-start(f32[2048]{0:T(1024)} %get-tuple-element.135) | copy-start | bytes 24580
  479.6 7.9 %copy-start.27 = (f32[1,2048]{1,0:T(1,128)S(1)}, f32[1,2048]{1,0:T(1,128)}, u32[]{:S(2)}) copy-start(f32[1,2048]{1,0:T(1,128)} %slice.262) | copy-start | bytes 24580
  479.6 8.0 %copy-start.21 = (f32[2048]{0:T(1024)S(1)}, f32[2048]{0:T(1024)}, u32[]{:S(2)}) copy-start(f32[2048]{0:T(1024)} %copy-done.20) | copy-start | bytes 24580
  479.6 8.0 %copy-start.26 = (f32[1,2048]{1,0:T(1,128)S(1)}, f32[1,2048]{1,0:T(1,128)}, u32[]{:S(2)}) copy-start(f32[1,2048]{1,0:T(1,128)} %slice.261) | copy-start | bytes 24580
  485.5 2.4 copy-start.19
  487.4 0.7 slice-start.2
  487.7 1.0 copy-start.6
  487.8 1.0 copy-start.17
  488.1 0.7 slice-start.1
  489.2 1.0 copy-start.2
  490.2 5.3 copy-start.15
  495.5 1.8 slice-start
  502.3 3.4 copy-start
  502.3 3.4 copy-start.4
  502.3 3.4 copy-start.13
  505.7 0.7 copy-start.25
  507.9 16.7 %copy-start.3 = (f32[256,2048]{1,0:T(8,128)S(1)}, f32[256,2048]{1,0:T(8,128)}, u32[]{:S(2)}) copy-start(f32[256,2048]{1,0:T(8,128)} %add.183) | copy-start | bytes 6291460
  524.6 25.5 %copy-start.23 = (f32[2048]{0:T(1024)S(1)}, f32[2048]{0:T(1024)}, u32[]{:S(2)}) copy-start(f32[2048]{0:T(1024)} %get-tuple-element.131) | copy-start | bytes 24580
  524.7 25.5 %copy-start.24 = (f32[2048]{0:T(1024)S(1)}, f32[2048]{0:T(1024)}, u32[]{:S(2)}) copy-start(f32[2048]{0:T(1024)} %get-tuple-element.142) | copy-start | bytes 24580
  524.7 25.5 %copy-start.28 = (f32[512]{0:T(512)S(1)}, f32[512]{0:T(512)}, u32[]{:S(2)}) copy-start(f32[512]{0:T(512)} %iota_add_fusion) | copy-start | bytes 6148
Sparse Core Ops, SparseCore 0:
  70.0 154.7 all-gather.4
  226.6 158.9 all-gather.6
where the time goes:
time: 566 us; the launch traced here: 564 us
  waiting for transfers between devices  300 us (53%)
  local copies, waits for them, and re-layouts  111 us (20%)
  matrix products  71.2 us (13%)
  other arithmetic  40.3 us (7%)
  blocking collectives  23.3 us (4%)
  between operations  14.7 us (3%)
    all_gather x1, waiting for transfers between devices, body(): all_rows = lax.all_gather(mr_out, 'ctx', axis=0, tiled=True)  161 us
    all_gather x1, waiting for transfers between devices, body(): gathered = lax.all_gather(gated, 'mp', axis=1, tiled=True)  138 us
    slice x34, local copies, waits for them, and re-layouts, body(): lax.associative_scan(link_pair, (decay_rows, drive_li), axis=0)  61.5 us
    conv_general_dilated x1, matrix products, body(): lax.conv_general_dilated(padded, kernel, (1,), 'VALID', dimension_numbers...  45.6 us
    pad x16, local copies, waits for them, and re-layouts, body(): lax.associative_scan(link_pair, (decay_rows, drive_li), axis=0)  35.5 us
    dot_general x1, matrix products, body(): summed = jnp.dot(gathered, all_rows, preferred_element_type=jnp.float32)  25.6 us
    all_gather x2, blocking collectives, carried_in(): pieces = jax.tree.map(lambda part: lax.all_gather(part, axis), value)  23.3 us
    add x16, other arithmetic, link_pair(): return (earlier[0] * later[0], later[0] * earlier[1] + later[1])  16.2 us
  transfers between devices with their start and end apart: 3, of which 2 were waited for; matrix products, arithmetic and copies ran while one was open for 1% of the time, Pallas kernels for 0%

commit v1 on v0

--- a/solution.py
+++ b/solution.py
@@ -2,6 +2,28 @@
 import jax.numpy as jnp
 from jax import lax
 from jax.sharding import PartitionSpec as P
+
+
+def laid_out(blocks, dim):
+    lengths = list(blocks.shape[1:])
+    lengths[dim] *= blocks.shape[0]
+    return jnp.moveaxis(blocks, 0, dim).reshape(lengths)
+
+
+def ring_gather(x, axis, dim):
+    size = lax.axis_size(axis)
+    pairs = [(i, (i + 1) % size) for i in range(size)]
+    back = [(b, a) for a, b in pairs]
+    lower, upper = ([], [])
+    for step in range(size - 1):
+        if step % 2 == 0:
+            lower.append(lax.ppermute(lower[-1] if lower else x, axis, pairs))
+        else:
+            upper.append(lax.ppermute(upper[-1] if upper else x, axis, back))
+    parts = jnp.stack([*lower[::-1], x, *upper])
+    shift = lax.axis_index(axis) - len(lower)
+    parts = parts[(jnp.arange(size) - shift) % size]
+    return laid_out(parts, dim)
 
 
 def passed_along(value, axis, by):
@@ -46,7 +68,7 @@
         precision=lax.Precision.HIGHEST,
     )[0]
     gated = (q_mr.astype(jnp.float32) * filtered).astype(jnp.bfloat16)
-    gathered = lax.all_gather(gated, "mp", axis=1, tiled=True)
+    gathered = ring_gather(gated, "mp", 1)
     all_rows = lax.all_gather(mr_out, "ctx", axis=0, tiled=True)
     summed = jnp.dot(gathered, all_rows, preferred_element_type=jnp.float32)
     mixed = (resid_in.astype(jnp.float32) + summed).astype(jnp.bfloat16)

time: 566 us -> 426 us (0.75)
  waiting for transfers between devices: 300 us -> 78.2 us
  blocking collectives: 23.3 us -> 67.5 us
  local copies, waits for them, and re-layouts: 111 us -> 135 us
  other arithmetic: 40.3 us -> 49.2 us
    all_gather x1, waiting for transfers between devices: 161 us -> 0.01 us  [body(): all_rows = lax.all_gather(mr_out, 'ctx', axis=0, tiled=True)]
    all_gather x1 -> x0, waiting for transfers between devices: 138 us -> none  [body(): gathered = lax.all_gather(gated, 'mp', axis=1, tiled=True)]
    ppermute x0 -> x3, waiting for transfers between devices: none -> 77.5 us  [the longest x2 77.5 us: ring_gather(): lower.append(lax.ppermute(lower[-1] if lower else x, axis, pairs))]
    all_gather x2, blocking collectives: 23.3 us -> 67.5 us  [carried_in(): pieces = jax.tree.map(lambda part: lax.all_gather(part, axis), value)]
    gather x0 -> x3, local copies, waits for them, and re-layouts: none -> 13.8 us  [ring_gather(): parts = parts[(jnp.arange(size) - shift) % size]]
    transpose x0 -> x1, local copies, waits for them, and re-layouts: none -> 11.5 us  [laid_out(): return jnp.moveaxis(blocks, 0, dim).reshape(lengths)]
    transpose x0 -> x1, other arithmetic: none -> 8.19 us  [laid_out(): return jnp.moveaxis(blocks, 0, dim).reshape(lengths)]
  transfers between devices with their start and end apart: 3 -> 5, of which waited for: 2 -> 2; matrix products, arithmetic and copies ran while one was open for 1% -> 23% of each run, Pallas kernels for 0% -> 0%
where the time goes in v1:
time: 426 us; the launch traced here: 424 us
  local copies, waits for them, and re-layouts  135 us (32%)
  waiting for transfers between devices  78.2 us (18%)
  matrix products  71 us (17%)
  blocking collectives  67.5 us (16%)
  other arithmetic  49.2 us (12%)
  between operations  14.8 us (3%)
  starting transfers between devices  7.84 us (2%)
    ppermute x2, waiting for transfers between devices, ring_gather(): lower.append(lax.ppermute(lower[-1] if lower else x, axis, pairs))  77.5 us
    all_gather x2, blocking collectives, carried_in(): pieces = jax.tree.map(lambda part: lax.all_gather(part, axis), value)  67.5 us
    slice x34, local copies, waits for them, and re-layouts, body(): lax.associative_scan(link_pair, (decay_rows, drive_li), axis=0)  61 us
    conv_general_dilated x1, matrix products, body(): lax.conv_general_dilated(padded, kernel, (1,), 'VALID', dimension_numbers...  45.6 us
    pad x16, local copies, waits for them, and re-layouts, body(): lax.associative_scan(link_pair, (decay_rows, drive_li), axis=0)  35.2 us
    dot_general x1, matrix products, body(): summed = jnp.dot(gathered, all_rows, preferred_element_type=jnp.float32)  25.4 us
    add x16, other arithmetic, link_pair(): return (earlier[0] * later[0], later[0] * earlier[1] + later[1])  15.7 us
    gather x3, local copies, waits for them, and re-layouts, ring_gather(): parts = parts[(jnp.arange(size) - shift) % size]  13.8 us
  transfers between devices with their start and end apart: 5, of which 2 were waited for; matrix products, arithmetic and copies ran while one was open for 23% of the time, Pallas kernels for 0%

profile of v1, /device:TPU:0, one launch (start us, length us, event | category | flops | bytes accessed | tf_op | source)
XLA Modules:
  0.0 423.8 jit_solution(3130670643961963972)
XLA Ops:
  7.9 3.1 multiply_convert_fusion.1
  11.9 3.2 collective-permute-start
  15.1 5.2 %rev.3 = f32[128,2048]{1,0:T(8,128)} reverse(f32[128,2048]{1,0:T(8,128)S(1)} %copy-done.4), dimensions={0} | reverse | bytes 2097152 | tf_op jit(solution)/shard_map/rev | solution.py:60
  20.3 1.9 maximum_bitcast_fusion.1
  22.2 45.6 %fusion = f32[1,512,2048]{2,0,1:T(1,128)S(1)} fusion(bf16[1,639,2048]{2,1,0:T(8,128)(2,1)S(1)} %maximum_bitcast_fusion.1, f32[128,1,2048]{2,0,1:T(8,128)S(1)} %bitcast.33), kind=kOutput, calls=%fused_computation.7 | convolution fusion | flops 1610612736 | bytes 7860224 | tf_op jit(solution)/shard_map/conv_general_dilated | solution.py:61
  67.8 2.3 fusion.2
  70.2 2.5 collective-permute-start.1
  72.7 2.1 collective-permute-start.3
  74.8 45.4 %collective-permute-done.1 = bf16[512,2048]{1,0:T(8,128)(2,1)} collective-permute-done((bf16[512,2048]{1,0:T(8,128)(2,1)S(1)}, bf16[512,2048]{1,0:T(8,128)(2,1)}, u32[]{:S(2)}, u32[]{:S(2)}) %collective-permute-start.1) | collective-permute-done | bytes 2097184 | tf_op jit(solution)/shard_map/ppermute | solution.py:20
  120.9 54.5 %all-gather = f32[16384]{0:T(1024)S(1)} all-gather(f32[2048]{0:T(1024)S(1)} %get-tuple-element.141), channel_id=2, replica_groups=mesh['ctx'=8,'mp'=4] {'ctx'}, dimensions={0}, use_global_device_ids=true | all-gather | bytes 73728 | tf_op jit(solution)/shard_map/all_gather | solution.py:37
  176.7 32.1 %collective-permute-done.2 = bf16[512,2048]{1,0:T(8,128)(2,1)} collective-permute-done((bf16[512,2048]{1,0:T(8,128)(2,1)}, bf16[512,2048]{1,0:T(8,128)(2,1)}, u32[]{:S(2)}, u32[]{:S(2)}) %collective-permute-start.2) | collective-permute-done | bytes 2097184 | tf_op jit(solution)/shard_map/ppermute | solution.py:20
  208.8 3.8 pad_maximum_fusion
  212.6 3.8 fusion.18
  216.4 5.0 %gather_fusion = bf16[4,512,1024]{2,1,0:T(8,128)(2,1)} fusion(bf16[4,512,1024]{2,1,0:T(8,128)(2,1)} %get-tuple-element.127, s32[1024]{0:T(1024)S(1)} %pad_clamp_fusion), kind=kCustom, calls=%fused_computation | custom fusion | bytes 8388624 | tf_op jit(solution)/shard_map/gather | solution.py:25
  221.4 5.0 %gather_fusion.1 = bf16[4,512,1024]{2,1,0:T(8,128)(2,1)} fusion(bf16[4,512,1024]{2,1,0:T(8,128)(2,1)} %get-tuple-element.128, s32[1024]{0:T(1024)S(1)} %pad_clamp_fusion), kind=kCustom, calls=%fused_computation.1 | custom fusion | bytes 8388624 | tf_op jit(solution)/shard_map/gather | solution.py:25
  226.4 8.2 %maximum_bitcast_fusion = bf16[512,4,2048]{2,0,1:T(8,128)(2,1)} fusion(bf16[4,512,1024]{2,1,0:T(8,128)(2,1)} %gather_fusion.1, bf16[4,512,1024]{2,1,0:T(8,128)(2,1)} %gather_fusion), kind=kLoop, calls=%fused_computation.6 | loop fusion | flops 16777216 | bytes 16777216 | tf_op jit(solution)/shard_map/transpose | solution.py:10
  234.6 11.5 %copy.18 = bf16[512,4,2048]{0,2,1:T(8,128)(2,1)} copy(bf16[512,4,2048]{2,0,1:T(8,128)(2,1)} %maximum_bitcast_fusion) | data formatting | bytes 16777216 | tf_op jit(solution)/shard_map/transpose | solution.py:10
  246.1 25.4 %convert_multiply_fusion = (f32[512,2048]{1,0:T(8,128)}, bf16[512,2048]{1,0:T(8,128)(2,1)}) fusion(bf16[512,2048]{1,0:T(8,128)(2,1)S(1)} %copy-done.33, bf16[512,8192]{0,1:T(8,128)(2,1)} %bitcast.31, bf16[8192,2048]{1,0:T(8,128)(2,1)} %all-gather.4.cloned.1.call-done, bf16[512,2048]{1,0:T(8,128)(2,1)} %param.12), kind=kOutput, calls=%fused_computation.12 | convolution fusion | flops 17186160640 | bytes 52428800 | tf_op jit(solution)/shard_map/dot_general | solution.py:73
  271.6 9.8 %slice.199 = f32[256,2048]{1,0:T(8,128)} slice(f32[512,2048]{1,0:T(8,128)} %get-tuple-element.145), slice={[0:511:2], [0:2048:1]} | slice | bytes 4194304 | tf_op jit(solution)/shard_map/slice | solution.py:78
  281.4 9.8 %slice.200 = f32[256,2048]{1,0:T(8,128)} slice(f32[512,2048]{1,0:T(8,128)} %get-tuple-element.145), slice={[1:512:2], [0:2048:1]} | slice | bytes 4194304 | tf_op jit(solution)/shard_map/slice | solution.py:78
  291.2 2.6 multiply_add_fusion
  293.7 3.3 slice.204
  297.0 2.8 slice.205
  299.8 1.7 multiply_add_fusion.1
  301.5 1.6 slice.209
  303.1 1.5 slice.210
  304.6 2.1 multiply_add_fusion.2
  306.6 1.7 slice.214
  308.3 1.7 slice.215
  314.7 1.5 multiply_add_fusion.5
  316.2 1.5 slice.229
  317.7 1.5 slice.230
  319.2 1.4 multiply_add_fusion.6
  323.3 1.5 slice.242
  327.8 1.5 slice.250
  329.4 3.0 slice.252
  332.4 10.1 %slice.254 = f32[255,2048]{1,0:T(8,128)} slice(f32[512,2048]{1,0:T(8,128)} %get-tuple-element.145), slice={[2:512:2], [0:2048:1]} | slice | bytes 4177920 | tf_op jit(solution)/shard_map/slice | solution.py:78
  342.5 1.4 slice.261
  346.3 1.4 fusion.4
  348.9 4.2 pad.69
  353.1 4.8 %pad.70 = f32[256,2048]{1,0:T(8,128)} pad(f32[128,2048]{1,0:T(8,128)S(1)} %add.207, f32[]{:T(128)} %constant.58.clone.1), padding=1_0_1x0_0_0 | pad | bytes 3145732 | tf_op jit(solution)/shard_map/pad | solution.py:78
  357.9 3.2 add.209
  361.1 16.5 %pad.72 = f32[512,2048]{1,0:T(8,128)} pad(f32[256,2048]{1,0:T(8,128)} %add.209, f32[]{:T(128)} %constant.58.clone.1), padding=1_0_1x0_0_0 | pad | bytes 6291460 | tf_op jit(solution)/shard_map/pad | solution.py:78
  377.6 2.8 fusion.3
  380.8 9.0 %pad.71 = f32[512,2048]{1,0:T(8,128)} pad(f32[256,2048]{1,0:T(8,128)S(1)} %pad_maximum_fusion.1, f32[]{:T(128)} %constant.58.clone.1), padding=0_1_1x0_0_0 | pad | bytes 6291460 | tf_op jit(solution)/shard_map/pad | solution.py:78
  390.7 13.0 %all-gather.1 = f32[8,1,2048]{2,1,0:T(1,128)S(1)} all-gather(f32[1,1,2048]{2,1,0:T(1,128)S(1)} %add_bitcast_fusion), channel_id=1, replica_groups=mesh['ctx'=8,'mp'=4] {'ctx'}, dimensions={0}, use_global_device_ids=true | all-gather | bytes 73728 | tf_op jit(solution)/shard_map/all_gather | solution.py:37
  403.7 6.3 %while.14 = (s32[]{:T(128)}, f32[2048]{0:T(1024)S(1)}, s32[]{:T(128)}, f32[8,2048]{1,0:T(8,128)}, f32[8,2048]{1,0:T(8,128)S(1)}, /*index=5*/s32[]{:T(128)}, s32[]{:T(128)}) while((s32[]{:T(128)}, f32[2048]{0:T(1024)S(1)}, s32[]{:T(128)}, f32[8,2048]{1,0:T(8,128)}, f32[8,2048]{1,0:T(8,128)S(1)}, /*index=5*/s32[]{:T(128)}, ...), condition=%wide.region_1.2_spmd.clone, body=%wide.region_0.1_spmd.clone.sunk | while | flops 8196 | bytes 65637 | solution.py:46
  410.0 6.9 %multiply_convert_fusion = bf16[512,2048]{1,0:T(8,128)(2,1)} fusion(f32[512,2048]{1,0:T(8,128)} %pad.71, f32[512,2048]{1,0:T(8,128)} %pad.72, bf16[512,2048]{1,0:T(8,128)(2,1)} %param.18, f32[2048]{0:T(1024)S(1)} %get-tuple-element.96, f32[512]{0:T(512)S(1)} %copy-done.30, f32[2048]{0:T(1024)S(1)} %copy-done.25, f32[2048]{0:T(1024)S(1)} %copy-done.24), kind=kLoop, calls=%fused_computation.11 | loop fusion | flops 8388608 | bytes 12609536 | tf_op jit(solution)/shard_map/convert_element_type | solution.py:88
  (153 shorter events, 24.5 us)
Async XLA Ops:
  7.2 239.0 %all-gather.4.cloned.1.call-start = ((), (), s32[]{:S(2)}) async-start(), calls=%async_computation | async-start | bytes 37748736 | tf_op jit(solution)/shard_map/all_gather | solution.py:72
  7.9 7.2 %copy-start.4 = (f32[128,2048]{1,0:T(8,128)S(1)}, f32[128,2048]{1,0:T(8,128)}, u32[]{:S(2)}) copy-start(f32[128,2048]{1,0:T(8,128)} %param.16) | copy-start | bytes 3145732
  11.9 8.4 %collective-permute-start = (bf16[127,2048]{1,0:T(8,128)(2,1)}, bf16[127,2048]{1,0:T(8,128)(2,1)}, u32[]{:S(2)}, u32[]{:S(2)}) collective-permute-start(bf16[127,2048]{1,0:T(8,128)(2,1)} %slice.260), channel_id=1, source_target_pairs={{0,4},{4,8},{8,12},{12,16},{16,20},{20,24},{24,28},{1,5},{5,9},{9,... | collective-permute-start | bytes 1560584 | tf_op jit(solution)/shard_map/ppermute | solution.py:32
  20.3 1.9 copy-start.5
  22.2 45.6 %copy-start.3 = (bf16[512,2048]{1,0:T(8,128)(2,1)S(1)}, bf16[512,2048]{1,0:T(8,128)(2,1)}, u32[]{:S(2)}) copy-start(bf16[512,2048]{1,0:T(8,128)(2,1)} %param.13) | copy-start | bytes 6291460
  67.8 52.4 %copy-start.31 = (f32[2048]{0:T(1024)S(1)}, f32[2048]{0:T(1024)}, u32[]{:S(2)}) copy-start(f32[2048]{0:T(1024)} %param.21) | copy-start | bytes 24580
  67.8 52.4 %copy-start.32 = (f32[2048]{0:T(1024)S(1)}, f32[2048]{0:T(1024)}, u32[]{:S(2)}) copy-start(f32[2048]{0:T(1024)} %param.20) | copy-start | bytes 24580
  70.2 50.0 %collective-permute-start.1 = (bf16[512,2048]{1,0:T(8,128)(2,1)S(1)}, bf16[512,2048]{1,0:T(8,128)(2,1)}, u32[]{:S(2)}, u32[]{:S(2)}) collective-permute-start(bf16[512,2048]{1,0:T(8,128)(2,1)S(1)} %fusion.2), channel_id=1, source_target_pairs={{0,1},{1,2},{2,3},{3,0},{4,5},{5,6},{6,7},{7,4},{8,9},{9,10},{10,1... | collective-permute-start | bytes 6291464 | tf_op jit(solution)/shard_map/ppermute | solution.py:20
  72.7 104.0 %collective-permute-start.3 = (bf16[512,2048]{1,0:T(8,128)(2,1)S(1)}, bf16[512,2048]{1,0:T(8,128)(2,1)}, u32[]{:S(2)}, u32[]{:S(2)}) collective-permute-start(bf16[512,2048]{1,0:T(8,128)(2,1)S(1)} %fusion.2), channel_id=1, source_target_pairs={{1,0},{2,1},{3,2},{0,3},{5,4},{6,5},{7,6},{4,7},{9,8},{10,9},{11,1... | collective-permute-start | bytes 6291464 | tf_op jit(solution)/shard_map/ppermute | solution.py:22
  120.2 88.6 %collective-permute-start.2 = (bf16[512,2048]{1,0:T(8,128)(2,1)}, bf16[512,2048]{1,0:T(8,128)(2,1)}, u32[]{:S(2)}, u32[]{:S(2)}) collective-permute-start(bf16[512,2048]{1,0:T(8,128)(2,1)} %collective-permute-done.1), channel_id=1, source_target_pairs={{0,1},{1,2},{2,3},{3,0},{4,5},{5,6},{6,7},{7,4},{8,9},{9,10},{10,1... | collective-permute-start | bytes 6291464 | tf_op jit(solution)/shard_map/ppermute | solution.py:20
  120.9 170.3 %copy-start.9 = (f32[2048]{0:T(1024)}, f32[2048]{0:T(1024)S(1)}, u32[]{:S(2)}) copy-start(f32[2048]{0:T(1024)S(1)} %get-tuple-element.140) | copy-start | bytes 24580
  120.9 179.0 %copy-start.11 = (f32[2048]{0:T(1024)}, f32[2048]{0:T(1024)S(1)}, u32[]{:S(2)}) copy-start(f32[2048]{0:T(1024)S(1)} %get-tuple-element.143) | copy-start | bytes 24580
  120.9 183.7 %copy-start.13 = (f32[2048]{0:T(1024)}, f32[2048]{0:T(1024)S(1)}, u32[]{:S(2)}) copy-start(f32[2048]{0:T(1024)S(1)} %get-tuple-element.142) | copy-start | bytes 24580
  120.9 189.1 %copy-start.15 = (f32[2048]{0:T(1024)}, f32[2048]{0:T(1024)S(1)}, u32[]{:S(2)}) copy-start(f32[2048]{0:T(1024)S(1)} %get-tuple-element.134) | copy-start | bytes 24580
  120.9 191.6 %copy-start.17 = (f32[2048]{0:T(1024)}, f32[2048]{0:T(1024)S(1)}, u32[]{:S(2)}) copy-start(f32[2048]{0:T(1024)S(1)} %get-tuple-element.135) | copy-start | bytes 24580
  234.6 11.6 %copy-start.33 = (bf16[512,2048]{1,0:T(8,128)(2,1)S(1)}, bf16[512,2048]{1,0:T(8,128)(2,1)}, u32[]{:S(2)}) copy-start(bf16[512,2048]{1,0:T(8,128)(2,1)} %param.19) | copy-start | bytes 6291460
  293.7 38.7 %copy-start = (f32[256,2048]{1,0:T(8,128)}, f32[256,2048]{1,0:T(8,128)S(1)}, u32[]{:S(2)}) copy-start(f32[256,2048]{1,0:T(8,128)S(1)} %multiply_add_fusion) | copy-start | bytes 6291460
  301.5 27.8 %copy-start.1 = (f32[128,2048]{1,0:T(8,128)}, f32[128,2048]{1,0:T(8,128)S(1)}, u32[]{:S(2)}) copy-start(f32[128,2048]{1,0:T(8,128)S(1)} %multiply_add_fusion.1) | copy-start | bytes 3145732
  326.7 17.6 %slice-start.3 = ((f32[8,2048]{1,0:T(8,128)}), f32[1,2048]{1,0:T(1,128)S(1)}, s32[]{:S(2)}) async-start(f32[8,2048]{1,0:T(8,128)} %multiply_add_fusion.5), calls=%async_computation.4 | async-start | bytes 16384 | tf_op jit(solution)/shard_map/slice | solution.py:78
  329.3 14.6 %copy-start.20 = (f32[2048]{0:T(1024)S(1)}, f32[2048]{0:T(1024)}, u32[]{:S(2)}) copy-start(f32[2048]{0:T(1024)} %get-tuple-element.139) | copy-start | bytes 24580
  329.3 14.6 %copy-start.22 = (f32[2,2048]{1,0:T(2,128)S(1)}, f32[2,2048]{1,0:T(2,128)}, u32[]{:S(2)}) copy-start(f32[2,2048]{1,0:T(2,128)} %slice.234) | copy-start | bytes 49156
  329.3 14.6 %copy-start.23 = (f32[2,2048]{1,0:T(2,128)S(1)}, f32[2,2048]{1,0:T(2,128)}, u32[]{:S(2)}) copy-start(f32[2,2048]{1,0:T(2,128)} %slice.235) | copy-start | bytes 49156
  329.3 14.6 %copy-start.27 = (f32[2048]{0:T(1024)S(1)}, f32[2048]{0:T(1024)}, u32[]{:S(2)}) copy-start(f32[2048]{0:T(1024)} %get-tuple-element.138) | copy-start | bytes 24580
  329.4 14.7 %copy-start.7 = (f32[4,2048]{1,0:T(4,128)S(1)}, f32[4,2048]{1,0:T(4,128)}, u32[]{:S(2)}) copy-start(f32[4,2048]{1,0:T(4,128)} %multiply_add_fusion.6) | copy-start | bytes 98308
  329.4 14.8 %copy-start.8 = (f32[3,2048]{1,0:T(4,128)S(1)}, f32[3,2048]{1,0:T(4,128)}, u32[]{:S(2)}) copy-start(f32[3,2048]{1,0:T(4,128)} %slice.242) | copy-start | bytes 73732
  329.4 14.8 %copy-start.21 = (f32[2048]{0:T(1024)S(1)}, f32[2048]{0:T(1024)}, u32[]{:S(2)}) copy-start(f32[2048]{0:T(1024)} %get-tuple-element.136) | copy-start | bytes 24580
  329.4 15.0 %copy-start.6 = (f32[7,2048]{1,0:T(8,128)S(1)}, f32[7,2048]{1,0:T(8,128)}, u32[]{:S(2)}) copy-start(f32[7,2048]{1,0:T(8,128)} %slice.244) | copy-start | bytes 172036
  329.4 15.0 %copy-start.19 = (f32[2048]{0:T(1024)S(1)}, f32[2048]{0:T(1024)}, u32[]{:S(2)}) copy-start(f32[2048]{0:T(1024)} %get-tuple-element.137) | copy-start | bytes 24580
  329.4 15.0 %copy-start.29 = (f32[1,2048]{1,0:T(1,128)S(1)}, f32[1,2048]{1,0:T(1,128)}, u32[]{:S(2)}) copy-start(f32[1,2048]{1,0:T(1,128)} %slice.266) | copy-start | bytes 24580
  329.4 15.1 %copy-start.18 = (f32[2048]{0:T(1024)S(1)}, f32[2048]{0:T(1024)}, u32[]{:S(2)}) copy-start(f32[2048]{0:T(1024)} %copy-done.17) | copy-start | bytes 24580
  332.4 12.2 %copy-start.28 = (f32[1,2048]{1,0:T(1,128)S(1)}, f32[1,2048]{1,0:T(1,128)}, u32[]{:S(2)}) copy-start(f32[1,2048]{1,0:T(1,128)} %slice.265) | copy-start | bytes 24580
  332.4 12.3 %copy-start.16 = (f32[2048]{0:T(1024)S(1)}, f32[2048]{0:T(1024)}, u32[]{:S(2)}) copy-start(f32[2048]{0:T(1024)} %copy-done.15) | copy-start | bytes 24580
  332.4 12.4 %slice-start.2 = ((f32[64,2048]{1,0:T(8,128)}), f32[1,2048]{1,0:T(1,128)S(1)}, s32[]{:S(2)}) async-start(f32[64,2048]{1,0:T(8,128)} %multiply_add_fusion.2), calls=%async_computation.3 | async-start | bytes 16384 | tf_op jit(solution)/shard_map/slice | solution.py:78
  344.6 1.0 copy-start.2
  344.6 1.0 copy-start.14
  344.7 1.0 slice-start.1
  345.6 0.7 copy-start.12
  345.8 2.0 slice-start
  361.1 16.5 %copy-start.10 = (f32[2048]{0:T(1024)S(1)}, f32[2048]{0:T(1024)}, u32[]{:S(2)}) copy-start(f32[2048]{0:T(1024)} %copy-done.9) | copy-start | bytes 24580
  377.6 2.8 copy-start.26
  380.7 29.3 %copy-start.24 = (f32[2048]{0:T(1024)S(1)}, f32[2048]{0:T(1024)}, u32[]{:S(2)}) copy-start(f32[2048]{0:T(1024)} %get-tuple-element.133) | copy-start | bytes 24580
  380.7 29.3 %copy-start.25 = (f32[2048]{0:T(1024)S(1)}, f32[2048]{0:T(1024)}, u32[]{:S(2)}) copy-start(f32[2048]{0:T(1024)} %get-tuple-element.144) | copy-start | bytes 24580
  380.7 29.3 %copy-start.30 = (f32[512]{0:T(512)S(1)}, f32[512]{0:T(512)}, u32[]{:S(2)}) copy-start(f32[512]{0:T(512)} %iota_add_fusion) | copy-start | bytes 6148
Sparse Core Ops, SparseCore 0:
  9.9 163.5 all-gather.3
